TPU v7x, 128 devices: a whole 4x4x4 slice. The times are simulated.
128 devices in a mesh: head: 2 (over y_hi), block: 2 (over y_lo), tok: 32 (over z, x, core).
Axes of the slice: x: 4, y: 4 (y_hi: 2, y_lo: 2; y = y_hi * 2 + y_lo), z: 4, core: 2. Of those that a mesh axis runs over, the one named last changes fastest.
Arguments:
- tokens: bfloat16 [2, 16384, 2048], P('block', 'tok'), may hold values from -6 to 6
- input_weight: bfloat16 [2048, 3, 2048], P(None, None, 'head'), may hold values from -0.125 to 0.125
- rate_weight: bfloat16 [2048, 4], P(None, 'head'), may hold values from -0.375 to 0.375
- fast_init: bfloat16 [4, 3, 512, 512], P('head'), may hold values from -0.25 to 0.25
- output_weight: bfloat16 [2048, 2048], P('head'), may hold values from -0.125 to 0.125
Outputs:
- mixed: bfloat16 [2, 16384, 2048], P('block', 'tok', 'head')
All inputs are finite; a program needn't handle non-finite values.
Results may differ from a plain program's by a relative error of at most 0.005.
Values sent between devices are 32-bit elements; how exact they have to be, the bound alone decides.
A program may use at most 128 MiB of HBM per device.

v0:
```python
import jax
import jax.numpy as jnp
from jax import lax
from jax.sharding import PartitionSpec as P

epsilon = 1e-06
step_size = 0.03
highest = lax.Precision.HIGHEST


def passed_along(block, axis, distance):
    devices = range(lax.axis_size(axis))
    route = [(i - distance, i) for i in devices if i - distance in devices]
    return lax.ppermute(block, axis, route)


def matmul(left, right):
    return jnp.dot(left, right, precision=highest, preferred_element_type=jnp.float32)


def normalize(values):
    return values / jnp.sqrt(jnp.mean(values * values, axis=-1, keepdims=True) + epsilon)


def fast_grad(weights, keys, targets):
    gate = matmul(keys, weights[0])
    upper = matmul(keys, weights[1])
    sigma = jax.nn.sigmoid(gate)
    active = gate * sigma
    hidden = active * upper
    grad_down = matmul(targets.T, hidden)
    back = matmul(targets, weights[2])
    grad_upper = matmul(keys.T, back * active)
    grad_gate = matmul(keys.T, back * upper * sigma * (1.0 + gate * (1.0 - sigma)))
    return jnp.stack([grad_gate, grad_upper, grad_down])


def fast_apply(weights, queries):
    gate = matmul(queries, weights[0])
    upper = matmul(queries, weights[1])
    hidden = gate * jax.nn.sigmoid(gate) * upper
    return normalize(matmul(hidden, weights[2].T))


def body(tokens, input_weight, rate_weight, fast_init, output_weight):
    block_count, tok_rows, model_width = tokens.shape
    head_count, _, head_dim, fast_dim = fast_init.shape
    start_weights = fast_init.astype(jnp.float32)
    flattened = tokens.reshape(block_count * tok_rows, model_width)
    projected = jnp.dot(
        flattened, input_weight.reshape(model_width, -1), preferred_element_type=jnp.float32
    )
    projected = projected.reshape(block_count, tok_rows, 3, head_count, head_dim)
    rates = jax.nn.softplus(jnp.dot(flattened, rate_weight, preferred_element_type=jnp.float32))
    rates = rates.reshape(block_count, tok_rows, head_count)
    queries = normalize(projected[:, :, 0])
    keys = normalize(projected[:, :, 1])
    targets = projected[:, :, 2] * rates[:, :, :, None]
    base_rms = jnp.sqrt(jnp.mean(start_weights * start_weights, axis=2, keepdims=True))
    head_grads = jax.vmap(fast_grad, in_axes=(0, 1, 1))
    position = lax.axis_index("block")
    groups = lax.axis_size("block")
    chosen = [start_weights]
    incoming = start_weights
    for section in range(groups):
        weights = incoming
        local = 0
        partial_value = head_grads(weights, keys[local], targets[local])
        pieces = lax.psum_scatter(partial_value, "tok", scatter_dimension=3, tiled=True)
        width = pieces.shape[3]
        squares = jnp.sum(pieces * pieces, axis=(2, 3))
        total_sq = lax.psum(squares, "tok")
        scale = jnp.sqrt(total_sq / (head_dim * fast_dim) + epsilon)[:, :, None, None]
        start = lax.axis_index("tok") * width
        own_weights = lax.dynamic_slice_in_dim(weights, start, width, 3)
        own_rms = lax.dynamic_slice_in_dim(base_rms, start, width, 3)
        moved = own_weights + step_size * pieces / scale
        fresh = moved * own_rms / jnp.sqrt(jnp.mean(moved * moved, axis=2, keepdims=True) + epsilon)
        weights = lax.all_gather(fresh, "tok", axis=3, tiled=True)
        chosen[local] = jnp.where(position == section, weights, chosen[local])
        if section + 1 < groups:
            incoming = passed_along(weights, "block", 1)
    head_apply = jax.vmap(fast_apply, in_axes=(0, 1), out_axes=1)
    joined = []
    local = 0
    applied = head_apply(chosen[local], queries[local])
    joined.append(applied.reshape(tok_rows, head_count * head_dim))
    joined = (
        jnp.stack(joined)
        .reshape(block_count * tok_rows, head_count * head_dim)
        .astype(jnp.bfloat16)
    )
    partial_out = jnp.dot(joined, output_weight, preferred_element_type=jnp.float32)
    partial_out = partial_out.reshape(block_count, tok_rows, model_width)
    return lax.psum_scatter(partial_out, "head", scatter_dimension=2, tiled=True).astype(
        jnp.bfloat16
    )


def solution(mesh):
    placed = (
        P("block", "tok", None),
        P(None, None, "head"),
        P(None, "head"),
        P("head", None, None, None),
        P("head", None),
    )
    return jax.shard_map(
        body, mesh=mesh, in_specs=placed, out_specs=P("block", "tok", "head"), check_vma=False
    )
```

profile of v0, /device:TPU:1, one launch (start us, length us, event | category | flops | bytes accessed | tf_op | source)
XLA Modules:
  0.0 829.3 jit_solution(6733005602457865795)
XLA Ops:
  6.5 17.1 %copy.79 = bf16[2048,3,1024]{0,2,1:T(8,128)(2,1)} copy(bf16[2048,3,1024]{2,0,1:T(8,128)(2,1)} %param.6) | data formatting | bytes 25165824 | tf_op args[1]
  23.6 9.5 %convolution_bitcast_fusion.1 = f32[1,512,3,2,512]{1,4,3,2,0:T(8,128)S(1)} fusion(bf16[3,2,512,2048]{3,2,1,0:T(8,128)(2,1)} %bitcast.143, bf16[1,512,2048]{2,1,0:T(8,128)(2,1)S(1)} %copy-done), kind=kOutput, calls=%fused_computation.5 | convolution fusion | flops 6442450944 | bytes 20971520 | tf_op jit(solution)/shard_map/dot_general | solution.py:50
  33.7 3.6 copy-done.4
  43.6 4.0 fusion.52
  47.5 4.5 fusion.47
  52.0 4.0 fusion.67
  56.0 3.3 maximum_bitcast_fusion
  59.3 10.3 %copy.87 = f32[2,3,512,512]{2,0,1,3:T(2,128)} copy(f32[2,3,512,512]{3,2,0,1:T(8,128)} %maximum_bitcast_fusion) | data formatting | bytes 12582912 | tf_op jit(solution)/shard_map/vmap()/transpose | solution.py:68
  73.0 3.5 convert_element_type.12
  78.4 110.3 %all-reduce.5.cloned.1.call-done = f32[2,3,512,512]{2,0,1,3:T(2,128)} async-done(((f32[2,3,512,512]{2,0,1,3:T(2,128)}), f32[2,3,512,512]{2,0,1,3:T(2,128)}) %all-reduce.5.cloned.1.call-update) | async-done | bytes 6291472
  189.9 62.7 %psum.14 = f32[2,3]{0,1:T(4,128)S(1)} all-reduce(f32[2,3]{0,1:T(4,128)S(1)} %get-tuple-element.9), channel_id=1, replica_groups=mesh['head'=2,'block'=2,'tok'=32] {'tok'}, use_global_device_ids=true, to_apply=%region_4.5 | all-reduce | flops 6 | bytes 48 | tf_op jit(solution)/shard_map/psum | solution.py:72
  255.7 49.4 %all-gather.3.cloned.1.call-done = f32[2,3,512,512]{2,0,1,3:T(2,128)} async-done(((f32[2,3,512,16]{2,0,1,3:T(2,128)}), f32[2,3,512,512]{2,0,1,3:T(2,128)}) %all-gather.3.cloned.1.call-update) | async-done | bytes 6291472 | tf_op jit(solution)/shard_map/all_gather | solution.py:79
  305.1 4.0 copy.91
  309.1 3.9 collective-permute-start
  313.0 133.8 %collective-permute-done = f32[2,3,512,512]{2,3,1,0:T(8,128)S(1)} collective-permute-done((f32[2,3,512,512]{2,3,1,0:T(8,128)S(1)}, f32[2,3,512,512]{2,3,1,0:T(8,128)S(1)}, u32[]{:S(2)}, u32[]{:S(2)}) %collective-permute-start) | collective-permute-done | bytes 6291488 | tf_op jit(solution)/shard_map/ppermute | solution.py:14
  446.8 10.1 %fusion.5 = f32[2,512,512]{2,1,0:T(8,128)S(1)} fusion(f32[2,3,512,512]{2,3,1,0:T(8,128)S(1)} %collective-permute-done, f32[1,512,3,2,512]{1,4,3,2,0:T(8,128)} %copy-done.2, f32[512,2]{0,1:T(2,128)S(1)} %compare_select_fusion), kind=kOutput, calls=%fused_computation.17 | convolution fusion | flops 3221749760 | bytes 6295552 | tf_op jit(solution)/shard_map/vmap()/dot_general | solution.py:18
  456.9 8.7 %fusion.3 = f32[2,512,512]{2,1,0:T(8,128)S(1)} fusion(f32[2,3,512,512]{2,3,1,0:T(8,128)S(1)} %collective-permute-done, f32[1,512,3,2,512]{1,4,3,2,0:T(8,128)} %copy-done.2, f32[512,2]{0,1:T(2,128)S(1)} %add_sqrt_fusion.2), kind=kOutput, calls=%fused_computation.13 | convolution fusion | flops 3221749760 | bytes 6295552 | tf_op jit(solution)/shard_map/vmap()/dot_general | solution.py:18
  465.6 4.0 fusion.62
  469.6 6.8 fusion.4
  476.4 4.5 fusion.57
  480.9 4.0 fusion.72
  484.9 3.4 maximum_bitcast_fusion.1
  488.3 10.3 %copy.98 = f32[2,3,512,512]{2,0,1,3:T(2,128)} copy(f32[2,3,512,512]{3,2,0,1:T(8,128)} %maximum_bitcast_fusion.1) | data formatting | bytes 12582912 | tf_op jit(solution)/shard_map/vmap()/transpose | solution.py:68
  498.7 115.7 %all-reduce.7.cloned.1.call-done = f32[2,3,512,512]{2,0,1,3:T(2,128)} async-done(((f32[2,3,512,512]{2,0,1,3:T(2,128)}), f32[2,3,512,512]{2,0,1,3:T(2,128)}) %all-reduce.7.cloned.1.call-update) | async-done | bytes 6291472
  615.6 62.7 %psum.15 = f32[2,3]{0,1:T(4,128)S(1)} all-reduce(f32[2,3]{0,1:T(4,128)S(1)} %get-tuple-element.7), channel_id=1, replica_groups=mesh['head'=2,'block'=2,'tok'=32] {'tok'}, use_global_device_ids=true, to_apply=%region_9.10 | all-reduce | flops 6 | bytes 48 | tf_op jit(solution)/shard_map/psum | solution.py:72
  681.9 48.9 %all-gather.5.cloned.1.call-done = f32[2,3,512,512]{2,0,1,3:T(2,128)} async-done(((f32[2,3,512,16]{2,0,1,3:T(2,128)}), f32[2,3,512,512]{2,0,1,3:T(2,128)}) %all-gather.5.cloned.1.call-update) | async-done | bytes 6291472 | tf_op jit(solution)/shard_map/all_gather | solution.py:79
  730.8 6.8 copy_select_fusion
  737.7 8.3 %fusion.2 = f32[2,512,512]{2,1,0:T(8,128)S(1)} fusion(f32[2,3,512,512]{2,3,1,0:T(8,128)S(1)} %copy_select_fusion, f32[1,512,3,2,512]{1,4,3,2,0:T(8,128)} %copy-done.2, f32[512,2]{0,1:T(2,128)S(1)} %add_sqrt_fusion.3), kind=kOutput, calls=%fused_computation.11 | convolution fusion | flops 3221749760 | bytes 6295552 | tf_op jit(solution)/shard_map/vmap()/dot_general | solution.py:18
  746.0 8.5 %fusion.1 = f32[2,512,512]{2,1,0:T(8,128)S(1)} fusion(f32[2,3,512,512]{2,3,1,0:T(8,128)S(1)} %copy_select_fusion, f32[1,512,3,2,512]{1,4,3,2,0:T(8,128)} %copy-done.2, f32[512,2]{0,1:T(2,128)S(1)} %add_sqrt_fusion.3), kind=kOutput, calls=%fused_computation.9 | convolution fusion | flops 3221749760 | bytes 6295552 | tf_op jit(solution)/shard_map/vmap()/dot_general | solution.py:18
  754.5 4.0 multiply_reduce_fusion.1
  758.8 4.3 convolution_bitcast_fusion
  763.2 56.7 %reduce-scatter.2.cloned.1.call-done = f32[1,512,1024]{2,1,0:T(8,128)} async-done(((f32[1,512,2048]{2,1,0:T(8,128)}), f32[1,512,1024]{2,1,0:T(8,128)}) %reduce-scatter.2.cloned.1.call-update) | async-done | bytes 2097168 | tf_op jit(solution)/shard_map/reduce_scatter | solution.py:95
  (58 shorter events, 23.6 us)
Async XLA Ops:
  6.5 17.1 %copy-start = (bf16[1,512,2048]{2,1,0:T(8,128)(2,1)S(1)}, bf16[1,512,2048]{2,1,0:T(8,128)(2,1)}, u32[]{:S(2)}) copy-start(bf16[1,512,2048]{2,1,0:T(8,128)(2,1)} %param.5) | copy-start | bytes 6291460
  6.5 182.2 %all-reduce.5.cloned.1.call-start = ((), (), s32[]{:S(2)}) async-start(), calls=%async_computation.4 | async-start | bytes 12582912
  33.1 18.9 %copy-start.2 = (f32[1,512,3,2,512]{1,4,3,2,0:T(8,128)}, f32[1,512,3,2,512]{1,4,3,2,0:T(8,128)S(1)}, u32[]{:S(2)}) copy-start(f32[1,512,3,2,512]{1,4,3,2,0:T(8,128)S(1)} %convolution_bitcast_fusion.1) | copy-start | bytes 18874372
  33.2 4.2 copy-start.4
  39.2 1.9 copy-start.6
  69.7 235.5 %all-gather.3.cloned.1.call-start = ((), (), s32[]{:S(2)}) async-start(), calls=%async_computation.1 | async-start | bytes 6488064 | tf_op jit(solution)/shard_map/all_gather | solution.py:79
  72.9 3.5 copy-start.7
  255.7 358.7 %all-reduce.7.cloned.1.call-start = ((), (), s32[]{:S(2)}) async-start(), calls=%async_computation.5 | async-start | bytes 12582912
  309.1 137.7 %collective-permute-start = (f32[2,3,512,512]{2,3,1,0:T(8,128)S(1)}, f32[2,3,512,512]{2,3,1,0:T(8,128)S(1)}, u32[]{:S(2)}, u32[]{:S(2)}) collective-permute-start(f32[2,3,512,512]{2,3,1,0:T(8,128)S(1)} %copy.91), channel_id=1, source_target_pairs={{0,32},{1,33},{2,34},{3,35},{4,36},{5,37},{6,38},{7,39},{8,40},{9,... | collective-permute-start | bytes 18874376 | tf_op jit(solution)/shard_map/ppermute | solution.py:14
  446.8 22.8 %copy-start.5 = (f32[2,3,512,512]{2,3,1,0:T(8,128)}, f32[2,3,512,512]{2,3,1,0:T(8,128)S(1)}, u32[]{:S(2)}) copy-start(f32[2,3,512,512]{2,3,1,0:T(8,128)S(1)} %collective-permute-done) | copy-start | bytes 18874372
  446.8 18.8 %slice-start = ((s8[6291456]{0:T(1024)(128)(4,1)}), s8[4194304]{0:T(1024)(128)(4,1)S(1)}, s32[]{:S(2)}) async-start(s8[6291456]{0:T(1024)(128)(4,1)} %bitcast.144), calls=%async_computation.6 | async-start | bytes 8388608
  456.9 8.7 %slice-start.1 = ((s8[6291456]{0:T(1024)(128)(4,1)}), s8[2097152]{0:T(1024)(128)(4,1)S(1)}, s32[]{:S(2)}) async-start(s8[6291456]{0:T(1024)(128)(4,1)} %bitcast.144), calls=%async_computation.7 | async-start | bytes 4194304
  498.6 232.2 %all-gather.5.cloned.1.call-start = ((), (), s32[]{:S(2)}) async-start(), calls=%async_computation.2 | async-start | bytes 6488064 | tf_op jit(solution)/shard_map/all_gather | solution.py:79
  681.4 138.5 %reduce-scatter.2.cloned.1.call-start = ((), (), s32[]{:S(2)}) async-start(), calls=%async_computation.3 | async-start | bytes 6291456 | tf_op jit(solution)/shard_map/reduce_scatter | solution.py:95
  754.5 4.4 copy-start.3
  763.1 59.4 %copy-start.1 = (bf16[1,512,2048]{2,1,0:T(8,128)(2,1)S(1)}, bf16[1,512,2048]{2,1,0:T(8,128)(2,1)}, u32[]{:S(2)}) copy-start(bf16[1,512,2048]{2,1,0:T(8,128)(2,1)} %param.5) | copy-start | bytes 6291460
Sparse Core Ops, SparseCore 0:
  69.8 118.8 all-reduce.4
  255.8 49.2 all-gather.2
  498.8 115.6 all-reduce.6
  681.5 49.2 all-gather.4
  763.3 56.5 reduce-scatter.1
where the time goes:
time: 833 us; the launch traced here: 829 us
  waiting for transfers between devices  515 us (62%)
  blocking collectives  125 us (15%)
  matrix products  91.2 us (11%)
  local copies, waits for them, and re-layouts  51 us (6%)
  other arithmetic  28.1 us (3%)
  between operations  14.3 us (2%)
    unnamed x7, waiting for transfers between devices  226 us
    ppermute x1, waiting for transfers between devices, passed_along(): return lax.ppermute(block, axis, route)  134 us
    psum x2, blocking collectives, body(): total_sq = lax.psum(squares, 'tok')  125 us
    all_gather x2, waiting for transfers between devices, body(): weights = lax.all_gather(fresh, 'tok', axis=3, tiled=True)  98.3 us
    dot_general x15, matrix products, matmul(): jnp.dot(left, right, precision=highest, preferred_element_type=jnp.float32)  76.7 us
    reduce_scatter x1, waiting for transfers between devices, body(): lax.psum_scatter(partial_out, 'head', scatter_dimension=2, tiled=True)  56.7 us
    unnamed x23, local copies, waits for them, and re-layouts  24.5 us
    transpose x2, local copies, waits for them, and re-layouts, body(): partial_value = head_grads(weights, keys[local], targets[local])  20.6 us
  transfers between devices with their start and end apart: 6, of which 6 were waited for; matrix products, arithmetic and copies ran while one was open for 1% of the time, Pallas kernels for 0%

commit v1 on v0

--- a/solution.py
+++ b/solution.py
@@ -2,6 +2,7 @@
 import jax.numpy as jnp
 from jax import lax
 from jax.sharding import PartitionSpec as P
+from jax.lax import all_to_all, axis_size
 
 epsilon = 1e-06
 step_size = 0.03
@@ -76,7 +77,8 @@
         own_rms = lax.dynamic_slice_in_dim(base_rms, start, width, 3)
         moved = own_weights + step_size * pieces / scale
         fresh = moved * own_rms / jnp.sqrt(jnp.mean(moved * moved, axis=2, keepdims=True) + epsilon)
-        weights = lax.all_gather(fresh, "tok", axis=3, tiled=True)
+        val = jnp.stack([fresh for _ in range(axis_size("tok"))])
+        weights = jnp.concatenate(all_to_all(val, "tok", 0, 0), axis=3)
         chosen[local] = jnp.where(position == section, weights, chosen[local])
         if section + 1 < groups:
             incoming = passed_along(weights, "block", 1)

time: 833 us -> 900 us (1.080)
  blocking collectives: 125 us -> 206 us
  waiting for transfers between devices: 515 us -> 492 us
    all_gather x2 -> x0, waiting for transfers between devices: 98.3 us -> none  [body(): weights = lax.all_gather(fresh, 'tok', axis=3, tiled=True)]
    all_to_all x0 -> x1, blocking collectives: none -> 80.5 us  [body(): weights = jnp.concatenate(all_to_all(val, 'tok', 0, 0), axis=3)]
    all_to_all x0 -> x1, waiting for transfers between devices: none -> 72.8 us  [body(): weights = jnp.concatenate(all_to_all(val, 'tok', 0, 0), axis=3)]
    unnamed x7 -> x5, waiting for transfers between devices: 226 us -> 226 us
    unnamed x23 -> x27, local copies, waits for them, and re-layouts: 24.5 us -> 24.5 us
  transfers between devices with their start and end apart: 6 -> 5, of which waited for: 6 -> 5; matrix products, arithmetic and copies ran while one was open for 1% -> 1% of each run, Pallas kernels for 0% -> 0%
where the time goes in v1:
time: 900 us; the launch traced here: 896 us
  waiting for transfers between devices  492 us (55%)
  blocking collectives  206 us (23%)
  matrix products  87 us (10%)
  local copies, waits for them, and re-layouts  55.1 us (6%)
  other arithmetic  29 us (3%)
  between operations  14.3 us (2%)
  starting transfers between devices  13.1 us (1%)
    unnamed x5, waiting for transfers between devices  226 us
    ppermute x1, waiting for transfers between devices, passed_along(): return lax.ppermute(block, axis, route)  134 us
    psum x2, blocking collectives, body(): total_sq = lax.psum(squares, 'tok')  125 us
    all_to_all x1, blocking collectives, body(): weights = jnp.concatenate(all_to_all(val, 'tok', 0, 0), axis=3)  80.5 us
    all_to_all x1, waiting for transfers between devices, body(): weights = jnp.concatenate(all_to_all(val, 'tok', 0, 0), axis=3)  72.8 us
    dot_general x15, matrix products, matmul(): jnp.dot(left, right, precision=highest, preferred_element_type=jnp.float32)  72.5 us
    reduce_scatter x1, waiting for transfers between devices, body(): lax.psum_scatter(partial_out, 'head', scatter_dimension=2, tiled=True)  59.6 us
    unnamed x27, local copies, waits for them, and re-layouts  24.5 us
  transfers between devices with their start and end apart: 5, of which 5 were waited for; matrix products, arithmetic and copies ran while one was open for 1% of the time, Pallas kernels for 0%

profile of v1, /device:TPU:1, one launch (start us, length us, event | category | flops | bytes accessed | tf_op | source)
XLA Modules:
  0.0 896.5 jit_solution(4585231092210500032)
XLA Ops:
  6.5 17.1 %copy.83 = bf16[2048,3,1024]{0,2,1:T(8,128)(2,1)} copy(bf16[2048,3,1024]{2,0,1:T(8,128)(2,1)} %param.6) | data formatting | bytes 25165824 | tf_op args[1]
  23.6 9.5 %convolution_bitcast_fusion.1 = f32[1,512,3,2,512]{1,4,3,2,0:T(8,128)S(1)} fusion(bf16[3,2,512,2048]{3,2,1,0:T(8,128)(2,1)} %bitcast.152, bf16[1,512,2048]{2,1,0:T(8,128)(2,1)S(1)} %copy-done), kind=kOutput, calls=%fused_computation.5 | convolution fusion | flops 6442450944 | bytes 20971520 | tf_op jit(solution)/shard_map/dot_general | solution.py:51
  33.7 3.6 copy-done.6
  43.6 4.0 fusion.52
  47.5 4.5 fusion.47
  52.0 4.0 fusion.67
  59.3 10.3 %copy.91 = f32[2,3,512,512]{2,0,1,3:T(2,128)} copy(f32[2,3,512,512]{3,2,0,1:T(8,128)} %maximum_bitcast_fusion) | data formatting | bytes 12582912 | tf_op jit(solution)/shard_map/vmap()/transpose | solution.py:69
  73.0 3.5 convert_element_type.12
  78.4 110.3 %all-reduce.5.cloned.1.call-done = f32[2,3,512,512]{2,0,1,3:T(2,128)} async-done(((f32[2,3,512,512]{2,0,1,3:T(2,128)}), f32[2,3,512,512]{2,0,1,3:T(2,128)}) %all-reduce.5.cloned.1.call-update) | async-done | bytes 6291472
  189.9 62.7 %psum.14 = f32[2,3]{0,1:T(4,128)S(1)} all-reduce(f32[2,3]{0,1:T(4,128)S(1)} %get-tuple-element.9), channel_id=1, replica_groups=mesh['head'=2,'block'=2,'tok'=32] {'tok'}, use_global_device_ids=true, to_apply=%region_4.5 | all-reduce | flops 6 | bytes 48 | tf_op jit(solution)/shard_map/psum | solution.py:73
  255.6 80.5 %all_to_all.10 = f32[32,2,3,512,16]{3,4,2,1,0:T(8,128)S(1)} all-to-all(f32[32,2,3,512,16]{3,4,2,1,0:T(8,128)S(1)} %stack.24), channel_id=1, replica_groups=mesh['head'=2,'block'=2,'tok'=32] {'tok'}, dimensions={0} | all-to-all | bytes 12582912 | tf_op jit(solution)/shard_map/all_to_all | solution.py:81
  337.5 3.9 collective-permute-start
  341.4 133.6 %collective-permute-done = f32[2,3,512,512]{2,3,1,0:T(8,128)S(1)} collective-permute-done((f32[2,3,512,512]{2,3,1,0:T(8,128)S(1)}, f32[2,3,512,512]{2,3,1,0:T(8,128)S(1)}, u32[]{:S(2)}, u32[]{:S(2)}) %collective-permute-start) | collective-permute-done | bytes 6291488 | tf_op jit(solution)/shard_map/ppermute | solution.py:15
  475.1 6.8 fusion.5
  481.9 7.0 fusion.3
  488.9 4.0 fusion.62
  492.9 6.8 fusion.4
  499.7 4.5 fusion.57
  504.2 4.0 fusion.72
  508.2 3.4 maximum_bitcast_fusion.1
  511.6 10.3 %copy.101 = f32[2,3,512,512]{2,0,1,3:T(2,128)} copy(f32[2,3,512,512]{3,2,0,1:T(8,128)} %maximum_bitcast_fusion.1) | data formatting | bytes 12582912 | tf_op jit(solution)/shard_map/vmap()/transpose | solution.py:69
  521.9 115.7 %all-reduce.7.cloned.1.call-done = f32[2,3,512,512]{2,0,1,3:T(2,128)} async-done(((f32[2,3,512,512]{2,0,1,3:T(2,128)}), f32[2,3,512,512]{2,0,1,3:T(2,128)}) %all-reduce.7.cloned.1.call-update) | async-done | bytes 6291472
  638.8 62.7 %psum.15 = f32[2,3]{0,1:T(4,128)S(1)} all-reduce(f32[2,3]{0,1:T(4,128)S(1)} %get-tuple-element.7), channel_id=1, replica_groups=mesh['head'=2,'block'=2,'tok'=32] {'tok'}, use_global_device_ids=true, to_apply=%region_9.10 | all-reduce | flops 6 | bytes 48 | tf_op jit(solution)/shard_map/psum | solution.py:73
  707.2 8.7 all-to-all-start.1
  716.4 72.8 %all-to-all-done.1 = f32[32,2,3,512,16]{3,4,2,1,0:T(8,128)} async-done(((f32[32,2,3,512,16]{3,4,2,1,0:T(8,128)}), f32[32,2,3,512,16]{3,4,2,1,0:T(8,128)}, u32[]{:S(2)}, u32[]{:S(2)}) %all-to-all-start.1) | async-done | bytes 6291488 | tf_op jit(solution)/shard_map/all_to_all | solution.py:81
  789.2 4.2 copy.104
  793.4 7.7 bitcast_select_fusion
  801.1 9.1 %fusion.2 = f32[2,512,512]{2,1,0:T(8,128)S(1)} fusion(f32[2,3,512,512]{2,3,1,0:T(8,128)} %bitcast_select_fusion, f32[1,512,3,2,512]{1,4,3,2,0:T(8,128)} %copy-done.3, f32[512,2]{0,1:T(2,128)S(1)} %add_sqrt_fusion.3), kind=kOutput, calls=%fused_computation.11 | convolution fusion | flops 3221749760 | bytes 6295552 | tf_op jit(solution)/shard_map/vmap()/dot_general | solution.py:19
  810.2 8.5 fusion.1
  818.7 4.0 multiply_reduce_fusion.1
  823.0 4.3 convolution_bitcast_fusion
  827.4 59.6 %reduce-scatter.2.cloned.1.call-done = f32[1,512,1024]{2,1,0:T(8,128)} async-done(((f32[1,512,2048]{2,1,0:T(8,128)}), f32[1,512,1024]{2,1,0:T(8,128)}) %reduce-scatter.2.cloned.1.call-update) | async-done | bytes 2097168 | tf_op jit(solution)/shard_map/reduce_scatter | solution.py:97
  (60 shorter events, 30.7 us)
Async XLA Ops:
  6.5 17.1 %copy-start = (bf16[1,512,2048]{2,1,0:T(8,128)(2,1)S(1)}, bf16[1,512,2048]{2,1,0:T(8,128)(2,1)}, u32[]{:S(2)}) copy-start(bf16[1,512,2048]{2,1,0:T(8,128)(2,1)} %param.5) | copy-start | bytes 6291460
  6.5 182.2 %all-reduce.5.cloned.1.call-start = ((), (), s32[]{:S(2)}) async-start(), calls=%async_computation.4 | async-start | bytes 12582912
  33.1 18.9 %copy-start.3 = (f32[1,512,3,2,512]{1,4,3,2,0:T(8,128)}, f32[1,512,3,2,512]{1,4,3,2,0:T(8,128)S(1)}, u32[]{:S(2)}) copy-start(f32[1,512,3,2,512]{1,4,3,2,0:T(8,128)S(1)} %convolution_bitcast_fusion.1) | copy-start | bytes 18874372
  33.2 4.2 copy-start.6
  39.2 1.9 copy-start.8
  69.7 568.0 %all-reduce.7.cloned.1.call-start = ((), (), s32[]{:S(2)}) async-start(), calls=%async_computation.5 | async-start | bytes 12582912
  72.9 3.5 copy-start.9
  255.6 219.5 %slice-start = ((s8[6291456]{0:T(1024)(128)(4,1)}), s8[4194304]{0:T(1024)(128)(4,1)S(1)}, s32[]{:S(2)}) async-start(s8[6291456]{0:T(1024)(128)(4,1)} %bitcast.153), calls=%async_computation.6 | async-start | bytes 8388608
  336.1 139.0 %slice-start.1 = ((s8[6291456]{0:T(1024)(128)(4,1)}), s8[2097152]{0:T(1024)(128)(4,1)S(1)}, s32[]{:S(2)}) async-start(s8[6291456]{0:T(1024)(128)(4,1)} %bitcast.153), calls=%async_computation.7 | async-start | bytes 4194304
  337.5 144.4 %copy-start.2 = (f32[32,2,3,512,16]{3,4,0,2,1:T(8,128)}, f32[32,2,3,512,16]{3,4,0,2,1:T(8,128)S(1)}, u32[]{:S(2)}) copy-start(f32[32,2,3,512,16]{3,4,0,2,1:T(8,128)S(1)} %copy.94) | copy-start | bytes 18874372
  337.5 137.6 %collective-permute-start = (f32[2,3,512,512]{2,3,1,0:T(8,128)S(1)}, f32[2,3,512,512]{2,3,1,0:T(8,128)S(1)}, u32[]{:S(2)}, u32[]{:S(2)}) collective-permute-start(f32[2,3,512,512]{2,3,1,0:T(8,128)S(1)} %bitcast.151), channel_id=1, source_target_pairs={{0,32},{1,33},{2,34},{3,35},{4,36},{5,37},{6,38},{7,39},{8,40},{9,... | collective-permute-start | bytes 18874376 | tf_op jit(solution)/shard_map/ppermute | solution.py:15
  475.1 17.8 %copy-start.7 = (f32[2,3,512,512]{2,3,1,0:T(8,128)}, f32[2,3,512,512]{2,3,1,0:T(8,128)S(1)}, u32[]{:S(2)}) copy-start(f32[2,3,512,512]{2,3,1,0:T(8,128)S(1)} %collective-permute-done) | copy-start | bytes 18874372
  707.2 82.0 %all-to-all-start.1 = ((f32[32,2,3,512,16]{3,4,2,1,0:T(8,128)}), f32[32,2,3,512,16]{3,4,2,1,0:T(8,128)}, u32[]{:S(2)}, u32[]{:S(2)}) async-start(f32[32,2,3,512,16]{3,4,2,1,0:T(8,128)} %stack.29), calls=%async_computation.1 | async-start | bytes 12582912 | tf_op jit(solution)/shard_map/all_to_all | solution.py:81
  715.9 171.2 %reduce-scatter.2.cloned.1.call-start = ((), (), s32[]{:S(2)}) async-start(), calls=%async_computation.3 | async-start | bytes 6291456 | tf_op jit(solution)/shard_map/reduce_scatter | solution.py:97
  801.1 9.1 %copy-start.5 = (f32[2,3,512,512]{2,3,1,0:T(8,128)S(1)}, f32[2,3,512,512]{2,3,1,0:T(8,128)}, u32[]{:S(2)}) copy-start(f32[2,3,512,512]{2,3,1,0:T(8,128)} %bitcast_select_fusion) | copy-start | bytes 18874372
  818.7 4.3 copy-start.4
  827.4 62.4 %copy-start.1 = (bf16[1,512,2048]{2,1,0:T(8,128)(2,1)S(1)}, bf16[1,512,2048]{2,1,0:T(8,128)(2,1)}, u32[]{:S(2)}) copy-start(bf16[1,512,2048]{2,1,0:T(8,128)(2,1)} %param.5) | copy-start | bytes 6291460
Sparse Core Ops, SparseCore 0:
  69.8 118.8 all-reduce.4
  522.1 115.5 all-reduce.6
  827.5 59.4 reduce-scatter.1
